TPU v7x, 32 devices: a whole 2x2x4 slice. The times are simulated.
32 devices in a mesh: member: 2 (over core), grid: 16 (over z, y, x).
Axes of the slice: x: 2, y: 2, z: 4, core: 2. Of those that a mesh axis runs over, the one named last changes fastest.
Arguments:
- latent: bfloat16 [4, 32768, 512], P('member', 'grid'), may hold values from -80 to 80
- block_pick: int32 [16, 16], P('grid'), may hold values from 0 to 15
- obs_weight: bfloat16 [16, 16, 128, 128], P('grid'), may hold values from 0.0099487305 to 1
- obs_value: float32 [16, 16, 128, 128], P('grid'), may hold values from -6 to 6
- obs_count: int32 [16, 16], P('grid'), may hold values from 0 to 128, as said below
- w_in: bfloat16 [512, 512], replicated, may hold values from -0.25 to 0.25
- b_in: float32 [512], replicated, may hold values from -3 to 3
- w_out: bfloat16 [512, 128], replicated, may hold values from -0.25 to 0.25
- b_out: float32 [128], replicated, may hold values from -3 to 3
Outputs:
- latent_grad: float32 [4, 32768, 512], P('member', 'grid')
- loss_value: float32 [], replicated
Inputs may be any that keep to these rules, and one draw needn't show every extreme that they name: Entry [d, j] counts the live observations of those slots; the live ones are the first slots, k < obs_count[d, j].
All inputs are finite; a program needn't handle non-finite values.
Results may differ from a plain program's by a relative error of at most 0.0041.
Values may be sent and summed in bfloat16 or wider, within the bound.
A program may use at most 128 MiB of HBM per device.

v0:
```python
import jax
import jax.numpy as jnp
from jax import lax
from jax.sharding import PartitionSpec as P

SOFTEN = 0.1


def smooth_abs(value):
    return jnp.sqrt(value * value + SOFTEN * SOFTEN)


def silu_slope(pre_act):
    sigmoid_value = jax.nn.sigmoid(pre_act)
    return sigmoid_value * (1.0 + pre_act * (1.0 - sigmoid_value))


def per_device(latent, block_pick, obs_weight, obs_value, obs_count, w_in, b_in, w_out, b_out):
    members_here, points, feature_width = latent.shape
    peer_count = lax.axis_size("grid")
    slot_count = obs_weight.shape[2]
    block_size = obs_weight.shape[3]
    channels = obs_value.shape[3]
    members_all = members_here * lax.axis_size("member")
    block_count = points // block_size
    local_blocks = latent.reshape(members_here, block_count, block_size, feature_width)
    picked_ids = block_pick[0]
    block_onehot = (
        picked_ids[:, None] == jnp.arange(block_count, dtype=jnp.int32)[None, :]
    ).astype(jnp.bfloat16)
    weight_sum = jnp.sum(obs_weight[0], axis=2, keepdims=True, dtype=jnp.float32)
    norm_weight = (obs_weight[0] / weight_sum).astype(jnp.bfloat16)
    picked = local_blocks[:, picked_ids]
    interp = jnp.einsum(
        "jkp,mjpc->mjkc",
        norm_weight,
        lax.all_to_all(picked, "grid", split_axis=1, concat_axis=1, tiled=True),
        preferred_element_type=jnp.float32,
    ).astype(jnp.bfloat16)
    flat_rows = interp.reshape(members_here * peer_count * slot_count, feature_width)
    pre_act = jnp.dot(flat_rows, w_in, preferred_element_type=jnp.float32) + b_in
    hidden = jax.nn.silu(pre_act).astype(jnp.bfloat16)
    predicted = jnp.dot(hidden, w_out, preferred_element_type=jnp.float32) + b_out
    predicted = predicted.reshape(members_here, peer_count, slot_count, channels)
    all_members = lax.all_gather(predicted, "member", axis=0, tiled=True)
    target = obs_value[0]
    live_mask = (jnp.arange(slot_count, dtype=jnp.int32)[None, :] < obs_count[0][:, None]).astype(
        jnp.float32
    )
    obs_diff = predicted - target[None]
    pair_diff = predicted[:, None] - all_members[None]
    per_obs = smooth_abs(obs_diff) / members_all - jnp.sum(smooth_abs(pair_diff), axis=1) / (
        2.0 * members_all * (members_all - 1)
    )
    loss_part = jnp.sum(per_obs * live_mask[None, :, :, None])
    live_count = jnp.sum(live_mask)
    live_total = lax.psum(live_count, "grid")
    loss_total = lax.psum(loss_part, ("member", "grid"))
    loss_value = loss_total / (channels * live_total)
    grad_scale = peer_count * peer_count * slot_count / live_total
    slope_obs = obs_diff / smooth_abs(obs_diff)
    slope_pair = jnp.sum(pair_diff / smooth_abs(pair_diff), axis=1)
    grad_pred = (
        grad_scale
        * live_mask[None, :, :, None]
        * (slope_obs / members_all - slope_pair / (members_all * (members_all - 1.0)))
    ).astype(jnp.bfloat16)
    grad_hidden = jnp.einsum(
        "rv,hv->rh", grad_pred.reshape(-1, channels), w_out, preferred_element_type=jnp.float32
    )
    grad_act = (grad_hidden * silu_slope(pre_act)).astype(jnp.bfloat16)
    grad_interp = jnp.einsum(
        "rh,ch->rc", grad_act, w_in, preferred_element_type=jnp.float32
    ).astype(jnp.bfloat16)
    grad_interp = grad_interp.reshape(members_here, peer_count, slot_count, feature_width)
    contribution = jnp.einsum(
        "jkp,mjkc->mjpc", norm_weight, grad_interp, preferred_element_type=jnp.float32
    ).astype(jnp.bfloat16)
    returned = lax.all_to_all(contribution, "grid", split_axis=1, concat_axis=1, tiled=True)
    summed = jnp.einsum("mdpc,db->mbpc", returned, block_onehot, preferred_element_type=jnp.float32)
    latent_grad = summed.reshape(members_here, points, feature_width)
    return (latent_grad, loss_value)


def solution(mesh):
    in_specs = (
        P("member", "grid", None),
        P("grid", None),
        P("grid", None, None, None),
        P("grid", None, None, None),
        P("grid", None),
        P(),
        P(),
        P(),
        P(),
    )
    out_specs = (P("member", "grid", None), P())
    return jax.shard_map(
        per_device, mesh=mesh, in_specs=in_specs, out_specs=out_specs, check_vma=False
    )
```

profile of v0, /device:TPU:0, one launch (start us, length us, event | category | flops | bytes accessed | tf_op | source)
XLA Modules:
  0.0 332.6 jit_solution(2911062721672756190)
XLA Ops:
  7.2 0.0 copy-start
  7.2 0.7 fusion.26
  7.9 5.0 %gather_fusion = bf16[16,2,128,512]{3,2,1,0:T(8,128)(2,1)} fusion(bf16[2,16,128,512]{3,2,1,0:T(8,128)(2,1)} %bitcast.72, s32[1024]{0:T(1024)S(1)} %pad_clamp_fusion), kind=kCustom, calls=%fused_computation | custom fusion | bytes 8388672 | tf_op jit(solution)/shard_map/gather | solution.py:33
  12.9 0.0 copy-start.4
  12.9 8.5 %all-to-all-start = ((bf16[2,16,128,512]{3,2,0,1:T(8,128)(2,1)}), bf16[2,16,128,512]{3,2,0,1:T(8,128)(2,1)}, u32[]{:S(2)}, u32[]{:S(2)}) async-start(bf16[2,16,128,512]{3,2,0,1:T(8,128)(2,1)} %bitcast.70), calls=%async_computation | async-start | bytes 8388608 | tf_op jit(solution)/shard_map/all_to_all | solution.py:37
  21.5 0.0 all-gather.2.cloned.1.call-start
  21.5 0.0 copy-done.4
  21.5 0.2 convert_reduce_fusion
  21.7 79.5 %all-to-all-done = bf16[2,16,128,512]{3,2,0,1:T(8,128)(2,1)} async-done(((bf16[2,16,128,512]{3,2,0,1:T(8,128)(2,1)}), bf16[2,16,128,512]{3,2,0,1:T(8,128)(2,1)}, u32[]{:S(2)}, u32[]{:S(2)}) %all-to-all-start) | async-done | bytes 4194336 | tf_op jit(solution)/shard_map/all_to_all | solution.py:37
  101.2 3.5 %convert_bitcast_fusion.1 = bf16[2,16,128,512]{3,2,0,1:T(8,128)(2,1)S(1)} fusion(bf16[2,16,128,512]{3,2,0,1:T(8,128)(2,1)} %all-to-all-done, bf16[1,16,128,128]{3,2,1,0:T(8,128)(2,1)S(1)} %copy-done.4, f32[16,128]{1,0:T(8,128)S(1)} %convert_reduce_fusion), kind=kOutput, calls=%fused_computation.17 | convolution fusion | flops 539754496 | bytes 8921088 | tf_op jit(solution)/shard_map/jkp,mjpc->mjkc/dot_general | solution.py:34
  104.7 0.4 copy.18
  105.1 0.0 copy-done
  105.1 0.0 copy-start.8
  105.1 0.0 copy-start.9
  105.2 0.0 copy-start.10
  105.2 2.4 fusion.31
  107.6 0.0 copy-done.8
  107.6 0.0 copy-done.9
  107.6 0.0 copy-done.10
  107.6 0.0 copy-start.3
  107.6 0.0 copy-start.6
  107.7 4.1 %convolution_add_fusion = f32[4096,128]{1,0:T(8,128)} fusion(bf16[512,128]{1,0:T(8,128)(2,1)S(1)} %copy-done.8, f32[4096,512]{1,0:T(8,128)S(1)} %fusion.31, f32[512]{0:T(512)S(1)} %copy-done.9, f32[128]{0:T(128)S(1)} %copy-done.10), kind=kOutput, calls=%fused_computation.11 | convolution fusion | flops 549978112 | bytes 10619392 | tf_op jit(solution)/shard_map/dot_general | solution.py:43
  111.7 0.0 copy-done.3
  111.7 0.0 all-gather.2.cloned.1.call-update
  111.8 0.0 copy-done.6
  111.8 0.7 fusion.25
  112.4 55.0 %psum.14 = f32[]{:T(128)} all-reduce(f32[]{:T(128)} %fusion.25), channel_id=1, replica_groups=mesh['member'=2,'grid'=16] {'grid'}, use_global_device_ids=true, to_apply=%region_1.2 | all-reduce | flops 1 | bytes 8 | tf_op jit(solution)/shard_map/psum | solution.py:57
  168.1 0.1 fusion.21
  168.2 0.1 fusion.20
  168.2 0.0 all-gather.2.cloned.1.call-done
  168.2 7.3 %fusion.2 = (f32[2,16,128,128]{3,2,1,0:T(8,128)S(1)}, f32[2,16,128,128]{3,2,1,0:T(8,128)S(1)}) fusion(f32[4,16,128,128]{3,2,1,0:T(8,128)} %all-gather.2.cloned.1.call-done, f32[2,16,128,128]{3,2,1,0:T(8,128)} %bitcast.68), kind=kLoop, calls=%fused_computation.5 | loop fusion | flops 11534336 | bytes 10485760 | tf_op jit(solution)/shard_map/reduce_sum | solution.py:52
  175.5 0.0 copy-start.2
  175.5 0.0 copy-start.5
  175.6 0.7 broadcast_multiply_fusion
  176.3 0.8 copy-done.2
  177.1 0.3 copy-done.5
  177.4 2.5 fusion.14
  179.9 8.6 %convolution_convert_fusion = bf16[4096,512]{1,0:T(8,128)(2,1)} fusion(bf16[512,512]{1,0:T(8,128)(2,1)S(1)} %copy-done, f32[4096,512]{1,0:T(8,128)} %copy-done.3, bf16[4096,128]{1,0:T(8,128)(2,1)S(1)} %get-tuple-element.5, bf16[512,128]{1,0:T(8,128)(2,1)S(1)} %copy-done.8, f32[512]{0:T(512)S(1)} %copy-done.9), kind=kOutput, calls=%fused_computation.10 | convolution fusion | flops 2707423232 | bytes 14288896 | tf_op jit(solution)/shard_map/rh,ch->rc/dot_general | solution.py:72
  188.6 5.9 %convert_bitcast_fusion = bf16[2,16,128,512]{2,3,0,1:T(8,128)(2,1)} fusion(bf16[2,16,128,512]{3,2,1,0:T(8,128)(2,1)} %bitcast.80, bf16[1,16,128,128]{3,2,1,0:T(8,128)(2,1)S(1)} %copy-done.4, f32[16,128]{1,0:T(8,128)S(1)} %convert_reduce_fusion), kind=kOutput, calls=%fused_computation.16 | convolution fusion | flops 539754496 | bytes 8921088 | tf_op jit(solution)/shard_map/jkp,mjkc->mjpc/dot_general | solution.py:76
  194.4 6.4 %copy.20 = bf16[2,16,128,512]{3,2,0,1:T(8,128)(2,1)} copy(bf16[2,16,128,512]{2,3,0,1:T(8,128)(2,1)} %convert_bitcast_fusion) | data formatting | bytes 8388608 | tf_op jit(solution)/shard_map/convert_element_type | solution.py:78
  200.8 0.0 copy-start.7
  200.8 4.7 %all-to-all-start.1 = ((bf16[2,16,128,512]{3,2,0,1:T(8,128)(2,1)}), bf16[2,16,128,512]{3,2,0,1:T(8,128)(2,1)}, u32[]{:S(2)}, u32[]{:S(2)}) async-start(bf16[2,16,128,512]{3,2,0,1:T(8,128)(2,1)} %copy.20), calls=%async_computation.1 | async-start | bytes 8388608 | tf_op jit(solution)/shard_map/all_to_all | solution.py:79
  206.1 104.7 %psum.15 = f32[]{:T(128)} all-reduce(f32[]{:T(128)} %get-tuple-element.4), channel_id=1, replica_groups=mesh['member'=2,'grid'=16] {'member','grid'}, use_global_device_ids=true, to_apply=%region_6.7 | all-reduce | flops 1 | bytes 8 | tf_op jit(solution)/shard_map/psum | solution.py:58
  311.6 0.0 all-to-all-done.1
  311.6 0.0 copy-done.7
  311.6 4.7 %fusion.8 = f32[2,16,128,512]{3,1,2,0:T(8,128)S(1)} fusion(bf16[2,16,128,512]{3,2,0,1:T(8,128)(2,1)} %all-to-all-done.1, s32[16]{0:T(128)S(1)} %bitcast.79), kind=kOutput, calls=%fused_computation.18 | convolution fusion | flops 67109120 | bytes 12582976 | tf_op jit(solution)/shard_map/mdpc,db->mbpc/dot_general | solution.py:80
  316.3 0.0 copy-start.1
  316.3 8.3 %copy.22 = f32[2,16,128,512]{3,2,1,0:T(8,128)} copy(f32[2,16,128,512]{3,1,2,0:T(8,128)S(1)} %fusion.8) | data formatting | bytes 16777216 | tf_op jit(solution)/shard_map/mdpc,db->mbpc/transpose | solution.py:80
  324.6 0.0 copy-done.1
  (3 shorter events, 0.0 us)
Async XLA Ops:
  7.2 98.0 %copy-start = (bf16[512,512]{1,0:T(8,128)(2,1)S(1)}, bf16[512,512]{1,0:T(8,128)(2,1)}, u32[]{:S(2)}) copy-start(bf16[512,512]{1,0:T(8,128)(2,1)} %param.14) | copy-start | bytes 1572868
  12.9 8.6 %copy-start.4 = (bf16[1,16,128,128]{3,2,1,0:T(8,128)(2,1)S(1)}, bf16[1,16,128,128]{3,2,1,0:T(8,128)(2,1)}, u32[]{:S(2)}) copy-start(bf16[1,16,128,128]{3,2,1,0:T(8,128)(2,1)} %param.11) | copy-start | bytes 1572868
  12.9 88.3 %all-to-all-start = ((bf16[2,16,128,512]{3,2,0,1:T(8,128)(2,1)}), bf16[2,16,128,512]{3,2,0,1:T(8,128)(2,1)}, u32[]{:S(2)}, u32[]{:S(2)}) async-start(bf16[2,16,128,512]{3,2,0,1:T(8,128)(2,1)} %bitcast.70), calls=%async_computation | async-start | bytes 8388608 | tf_op jit(solution)/shard_map/all_to_all | solution.py:37
  21.5 146.8 %all-gather.2.cloned.1.call-start = ((), (), s32[]{:S(2)}) async-start(), calls=%async_computation.2 | async-start | bytes 6291456 | tf_op jit(solution)/shard_map/all_gather | solution.py:45
  105.1 2.5 copy-start.8
  105.1 2.5 copy-start.9
  105.2 2.5 copy-start.10
  107.6 4.1 %copy-start.3 = (f32[4096,512]{1,0:T(8,128)}, f32[4096,512]{1,0:T(8,128)S(1)}, u32[]{:S(2)}) copy-start(f32[4096,512]{1,0:T(8,128)S(1)} %fusion.31) | copy-start | bytes 25165828
  107.6 4.1 %copy-start.6 = (s32[1,16]{1,0:T(1,128)S(1)}, s32[1,16]{1,0:T(1,128)}, u32[]{:S(2)}) copy-start(s32[1,16]{1,0:T(1,128)} %param.13) | copy-start | bytes 196
  175.5 1.6 copy-start.2
  175.5 1.8 copy-start.5
  200.8 110.7 %copy-start.7 = (s32[1,16]{1,0:T(1,128)S(1)}, s32[1,16]{1,0:T(1,128)}, u32[]{:S(2)}) copy-start(s32[1,16]{1,0:T(1,128)} %param.10) | copy-start | bytes 196
  200.8 110.7 %all-to-all-start.1 = ((bf16[2,16,128,512]{3,2,0,1:T(8,128)(2,1)}), bf16[2,16,128,512]{3,2,0,1:T(8,128)(2,1)}, u32[]{:S(2)}, u32[]{:S(2)}) async-start(bf16[2,16,128,512]{3,2,0,1:T(8,128)(2,1)} %copy.20), calls=%async_computation.1 | async-start | bytes 8388608 | tf_op jit(solution)/shard_map/all_to_all | solution.py:79
  316.3 8.3 %copy-start.1 = (bf16[512,512]{1,0:T(8,128)(2,1)S(1)}, bf16[512,512]{1,0:T(8,128)(2,1)}, u32[]{:S(2)}) copy-start(bf16[512,512]{1,0:T(8,128)(2,1)} %param.14) | copy-start | bytes 1572868
Sparse Core Ops, SparseCore 0:
  111.9 28.1 all-gather.1
where the time goes:
time: 333 us
  blocking collectives  160 us (48%)
  waiting for transfers between devices  79.5 us (24%)
  matrix products  29.2 us (9%)
  local copies, waits for them, and re-layouts  21.3 us (6%)
  between operations  17.4 us (5%)
  starting transfers between devices  13.2 us (4%)
  other arithmetic  12.3 us (4%)
    psum x1, blocking collectives, per_device(): loss_total = lax.psum(loss_part, ('member', 'grid'))  105 us
    all_to_all x1, waiting for transfers between devices, per_device(): lax.all_to_all(picked, 'grid', split_axis=1, concat_axis=1, tiled=True)  79.5 us
    psum x1, blocking collectives, per_device(): live_total = lax.psum(live_count, 'grid')  55 us
    dot_general x1, matrix products, per_device(): jnp.einsum('rh,ch->rc', grad_act, w_in, preferred_element_type=jnp.float32)  8.64 us
    all_to_all x1, starting transfers between devices, per_device(): lax.all_to_all(picked, 'grid', split_axis=1, concat_axis=1, tiled=True)  8.52 us
    transpose x1, local copies, waits for them, and re-layouts, per_device(): jnp.einsum('mdpc,db->mbpc', returned, block_onehot, preferred_element_typ...  8.25 us
    reduce_sum x1, other arithmetic, per_device(): jnp.sum(smooth_abs(pair_diff), axis=1)  7.3 us
  transfers between devices with their start and end apart: 3, of which 1 were waited for; matrix products, arithmetic and copies ran while one was open for 0% of the time, Pallas kernels for 0%

commit v1 on v0

--- a/solution.py
+++ b/solution.py
@@ -31,11 +31,14 @@
     weight_sum = jnp.sum(obs_weight[0], axis=2, keepdims=True, dtype=jnp.float32)
     norm_weight = (obs_weight[0] / weight_sum).astype(jnp.bfloat16)
     picked = local_blocks[:, picked_ids]
+    cover_the_pools = lambda x_part: jnp.concatenate(
+        jax.lax.all_to_all(
+            jnp.stack(jnp.split(x_part, jax.lax.psum(1, "grid"), axis=1), axis=0), "grid", 0, 0
+        ),
+        axis=1,
+    )
     interp = jnp.einsum(
-        "jkp,mjpc->mjkc",
-        norm_weight,
-        lax.all_to_all(picked, "grid", split_axis=1, concat_axis=1, tiled=True),
-        preferred_element_type=jnp.float32,
+        "jkp,mjpc->mjkc", norm_weight, cover_the_pools(picked), preferred_element_type=jnp.float32
     ).astype(jnp.bfloat16)
     flat_rows = interp.reshape(members_here * peer_count * slot_count, feature_width)
     pre_act = jnp.dot(flat_rows, w_in, preferred_element_type=jnp.float32) + b_in

time: 333 us -> 353 us (1.060)
  local copies, waits for them, and re-layouts: 21.3 us -> 40.6 us
    unnamed x22 -> x39, local copies, waits for them, and re-layouts: 1.14 us -> 19.7 us
where the time goes in v1:
time: 353 us; the launch traced here: 352 us
  blocking collectives  160 us (45%)
  waiting for transfers between devices  79.5 us (23%)
  local copies, waits for them, and re-layouts  40.6 us (12%)
  matrix products  29.2 us (8%)
  between operations  17.4 us (5%)
  starting transfers between devices  13.2 us (4%)
  other arithmetic  12.3 us (3%)
    psum x1, blocking collectives, per_device(): loss_total = lax.psum(loss_part, ('member', 'grid'))  105 us
    all_to_all x1, waiting for transfers between devices, per_device(): jax.lax.all_to_all(jnp.stack(jnp.split(x_part, jax.lax.psum(1, 'grid'), a...  79.5 us
    psum x1, blocking collectives, per_device(): live_total = lax.psum(live_count, 'grid')  55 us
    unnamed x39, local copies, waits for them, and re-layouts  19.7 us
    dot_general x1, matrix products, per_device(): jnp.einsum('rh,ch->rc', grad_act, w_in, preferred_element_type=jnp.float32)  8.64 us
    all_to_all x1, starting transfers between devices, per_device(): jax.lax.all_to_all(jnp.stack(jnp.split(x_part, jax.lax.psum(1, 'grid'), a...  8.52 us
    transpose x1, local copies, waits for them, and re-layouts, per_device(): jnp.einsum('mdpc,db->mbpc', returned, block_onehot, preferred_element_typ...  8.25 us
    reduce_sum x1, other arithmetic, per_device(): jnp.sum(smooth_abs(pair_diff), axis=1)  7.3 us
  transfers between devices with their start and end apart: 3, of which 1 were waited for; matrix products, arithmetic and copies ran while one was open for 0% of the time, Pallas kernels for 0%

profile of v1, /device:TPU:0, one launch (start us, length us, event | category | flops | bytes accessed | tf_op | source)
XLA Modules:
  0.0 351.9 jit_solution(15275541808133023179)
XLA Ops:
  7.2 0.0 copy-start
  7.2 0.7 fusion.46
  7.9 5.0 %gather_fusion = bf16[16,2,128,512]{3,2,1,0:T(8,128)(2,1)} fusion(bf16[2,16,128,512]{3,2,1,0:T(8,128)(2,1)} %bitcast.159, s32[1024]{0:T(1024)S(1)} %pad_clamp_fusion), kind=kCustom, calls=%fused_computation | custom fusion | bytes 8388672 | tf_op jit(solution)/shard_map/gather | solution.py:33
  12.9 0.0 copy-start.3
  12.9 1.8 fusion.39
  14.7 1.7 fusion.38
  16.4 1.7 fusion.37
  18.1 1.7 fusion.36
  19.7 1.7 fusion.35
  21.4 1.7 fusion.34
  23.1 1.7 fusion.33
  24.8 1.7 fusion.32
  26.5 0.0 copy-done.3
  26.5 0.7 fusion.31
  27.2 0.7 fusion.30
  27.9 0.7 fusion.29
  28.7 0.7 fusion.28
  29.4 0.7 fusion.27
  30.1 0.7 fusion.26
  30.8 0.7 fusion.25
  31.5 0.7 fusion.24
  32.3 8.5 %all-to-all-start = ((bf16[16,2,1,128,512]{4,3,1,2,0:T(8,128)(2,1)}), bf16[16,2,1,128,512]{4,3,1,2,0:T(8,128)(2,1)}, u32[]{:S(2)}, u32[]{:S(2)}) async-start(bf16[16,2,1,128,512]{4,3,1,2,0:T(8,128)(2,1)} %fusion.24), calls=%async_computation | async-start | bytes 8388608 | tf_op jit(solution)/shard_map/all_to_all | solution.py:35
  40.8 0.0 all-gather.2.cloned.1.call-start
  40.9 0.0 copy-done.5
  40.9 0.2 convert_reduce_fusion
  41.1 79.5 %all-to-all-done = bf16[16,2,1,128,512]{4,3,1,2,0:T(8,128)(2,1)} async-done(((bf16[16,2,1,128,512]{4,3,1,2,0:T(8,128)(2,1)}), bf16[16,2,1,128,512]{4,3,1,2,0:T(8,128)(2,1)}, u32[]{:S(2)}, u32[]{:S(2)}) %all-to-all-start) | async-done | bytes 4194336 | tf_op jit(solution)/shard_map/all_to_all | solution.py:35
  120.6 3.5 convert_bitcast_fusion.1
  124.1 0.4 copy.50
  124.5 0.0 copy-done
  124.5 0.0 copy-start.9
  124.5 0.0 copy-start.10
  124.5 0.0 copy-start.11
  124.5 2.4 fusion.51
  127.0 0.0 copy-done.9
  127.0 0.0 copy-done.10
  127.0 0.0 copy-done.11
  127.0 0.0 copy-start.4
  127.0 0.0 copy-start.7
  127.0 4.1 %convolution_add_fusion = f32[4096,128]{1,0:T(8,128)} fusion(bf16[512,128]{1,0:T(8,128)(2,1)S(1)} %copy-done.9, f32[4096,512]{1,0:T(8,128)S(1)} %fusion.51, f32[512]{0:T(512)S(1)} %copy-done.10, f32[128]{0:T(128)S(1)} %copy-done.11), kind=kOutput, calls=%fused_computation.11 | convolution fusion | flops 549978112 | bytes 10619392 | tf_op jit(solution)/shard_map/dot_general | solution.py:46
  131.1 0.0 copy-done.4
  131.1 0.0 all-gather.2.cloned.1.call-update
  131.1 0.0 copy-done.7
  131.1 0.7 fusion.45
  131.8 55.0 %psum.14 = f32[]{:T(128)} all-reduce(f32[]{:T(128)} %fusion.45), channel_id=1, replica_groups=mesh['member'=2,'grid'=16] {'grid'}, use_global_device_ids=true, to_apply=%region_1.2 | all-reduce | flops 1 | bytes 8 | tf_op jit(solution)/shard_map/psum | solution.py:60
  187.4 0.1 fusion.41
  187.5 0.1 fusion.40
  187.6 7.3 %fusion.2 = (f32[2,16,128,128]{3,2,1,0:T(8,128)S(1)}, f32[2,16,128,128]{3,2,1,0:T(8,128)S(1)}) fusion(f32[4,16,128,128]{3,2,1,0:T(8,128)} %all-gather.2.cloned.1.call-done, f32[2,16,128,128]{3,2,1,0:T(8,128)} %bitcast.140), kind=kLoop, calls=%fused_computation.5 | loop fusion | flops 11534336 | bytes 10485760 | tf_op jit(solution)/shard_map/reduce_sum | solution.py:55
  194.9 0.0 copy-start.2
  194.9 0.0 copy-start.6
  194.9 0.7 broadcast_multiply_fusion
  195.7 0.8 copy-done.2
  196.5 0.3 copy-done.6
  196.8 2.5 fusion.18
  199.3 8.6 %convolution_convert_fusion = bf16[4096,512]{1,0:T(8,128)(2,1)} fusion(bf16[512,512]{1,0:T(8,128)(2,1)S(1)} %copy-done, f32[4096,512]{1,0:T(8,128)} %copy-done.4, bf16[4096,128]{1,0:T(8,128)(2,1)S(1)} %get-tuple-element.5, bf16[512,128]{1,0:T(8,128)(2,1)S(1)} %copy-done.9, f32[512]{0:T(512)S(1)} %copy-done.10), kind=kOutput, calls=%fused_computation.10 | convolution fusion | flops 2707423232 | bytes 14288896 | tf_op jit(solution)/shard_map/rh,ch->rc/dot_general | solution.py:75
  207.9 5.9 %convert_bitcast_fusion = bf16[2,16,128,512]{2,3,0,1:T(8,128)(2,1)} fusion(bf16[2,16,128,512]{3,2,1,0:T(8,128)(2,1)} %bitcast.167, bf16[1,16,128,128]{3,2,1,0:T(8,128)(2,1)S(1)} %copy-done.5, f32[16,128]{1,0:T(8,128)S(1)} %convert_reduce_fusion), kind=kOutput, calls=%fused_computation.18 | convolution fusion | flops 539754496 | bytes 8921088 | tf_op jit(solution)/shard_map/jkp,mjkc->mjpc/dot_general | solution.py:79
  213.8 6.4 %copy.52 = bf16[2,16,128,512]{3,2,0,1:T(8,128)(2,1)} copy(bf16[2,16,128,512]{2,3,0,1:T(8,128)(2,1)} %convert_bitcast_fusion) | data formatting | bytes 8388608 | tf_op jit(solution)/shard_map/convert_element_type | solution.py:81
  220.2 4.7 %all-to-all-start.1 = ((bf16[2,16,128,512]{3,2,0,1:T(8,128)(2,1)}), bf16[2,16,128,512]{3,2,0,1:T(8,128)(2,1)}, u32[]{:S(2)}, u32[]{:S(2)}) async-start(bf16[2,16,128,512]{3,2,0,1:T(8,128)(2,1)} %copy.52), calls=%async_computation.1 | async-start | bytes 8388608 | tf_op jit(solution)/shard_map/all_to_all | solution.py:82
  225.5 104.7 %psum.15 = f32[]{:T(128)} all-reduce(f32[]{:T(128)} %get-tuple-element.4), channel_id=1, replica_groups=mesh['member'=2,'grid'=16] {'member','grid'}, use_global_device_ids=true, to_apply=%region_6.7 | all-reduce | flops 1 | bytes 8 | tf_op jit(solution)/shard_map/psum | solution.py:61
  330.9 0.0 all-to-all-done.1
  330.9 0.0 copy-done.8
  330.9 4.7 %fusion.10 = f32[2,16,128,512]{3,1,2,0:T(8,128)S(1)} fusion(bf16[2,16,128,512]{3,2,0,1:T(8,128)(2,1)} %all-to-all-done.1, s32[16]{0:T(128)S(1)} %bitcast.166), kind=kOutput, calls=%fused_computation.20 | convolution fusion | flops 67109120 | bytes 12582976 | tf_op jit(solution)/shard_map/mdpc,db->mbpc/dot_general | solution.py:83
  335.7 0.0 copy-start.1
  335.7 8.3 %copy.54 = f32[2,16,128,512]{3,2,1,0:T(8,128)} copy(f32[2,16,128,512]{3,1,2,0:T(8,128)S(1)} %fusion.10) | data formatting | bytes 16777216 | tf_op jit(solution)/shard_map/mdpc,db->mbpc/transpose | solution.py:83
  343.9 0.0 copy-done.1
  (6 shorter events, 0.0 us)
Async XLA Ops:
  7.2 117.3 %copy-start = (bf16[512,512]{1,0:T(8,128)(2,1)S(1)}, bf16[512,512]{1,0:T(8,128)(2,1)}, u32[]{:S(2)}) copy-start(bf16[512,512]{1,0:T(8,128)(2,1)} %param.14) | copy-start | bytes 1572868
  12.9 13.6 %copy-start.3 = (bf16[16,2,128,512]{3,2,1,0:T(8,128)(2,1)S(1)}, bf16[16,2,128,512]{3,2,1,0:T(8,128)(2,1)}, u32[]{:S(2)}) copy-start(bf16[16,2,128,512]{3,2,1,0:T(8,128)(2,1)} %gather_fusion) | copy-start | bytes 12582916
  32.3 8.6 %copy-start.5 = (bf16[1,16,128,128]{3,2,1,0:T(8,128)(2,1)S(1)}, bf16[1,16,128,128]{3,2,1,0:T(8,128)(2,1)}, u32[]{:S(2)}) copy-start(bf16[1,16,128,128]{3,2,1,0:T(8,128)(2,1)} %param.11) | copy-start | bytes 1572868
  32.3 88.3 %all-to-all-start = ((bf16[16,2,1,128,512]{4,3,1,2,0:T(8,128)(2,1)}), bf16[16,2,1,128,512]{4,3,1,2,0:T(8,128)(2,1)}, u32[]{:S(2)}, u32[]{:S(2)}) async-start(bf16[16,2,1,128,512]{4,3,1,2,0:T(8,128)(2,1)} %fusion.24), calls=%async_computation | async-start | bytes 8388608 | tf_op jit(solution)/shard_map/all_to_all | solution.py:35
  40.8 146.8 %all-gather.2.cloned.1.call-start = ((), (), s32[]{:S(2)}) async-start(), calls=%async_computation.2 | async-start | bytes 6291456 | tf_op jit(solution)/shard_map/all_gather | solution.py:48
  124.5 2.5 copy-start.9
  124.5 2.5 copy-start.10
  124.5 2.5 copy-start.11
  127.0 4.1 %copy-start.4 = (f32[4096,512]{1,0:T(8,128)}, f32[4096,512]{1,0:T(8,128)S(1)}, u32[]{:S(2)}) copy-start(f32[4096,512]{1,0:T(8,128)S(1)} %fusion.51) | copy-start | bytes 25165828
  127.0 4.1 %copy-start.7 = (s32[1,16]{1,0:T(1,128)S(1)}, s32[1,16]{1,0:T(1,128)}, u32[]{:S(2)}) copy-start(s32[1,16]{1,0:T(1,128)} %param.13) | copy-start | bytes 196
  194.9 1.6 copy-start.2
  194.9 1.8 copy-start.6
  220.2 110.7 %copy-start.8 = (s32[1,16]{1,0:T(1,128)S(1)}, s32[1,16]{1,0:T(1,128)}, u32[]{:S(2)}) copy-start(s32[1,16]{1,0:T(1,128)} %param.10) | copy-start | bytes 196
  220.2 110.7 %all-to-all-start.1 = ((bf16[2,16,128,512]{3,2,0,1:T(8,128)(2,1)}), bf16[2,16,128,512]{3,2,0,1:T(8,128)(2,1)}, u32[]{:S(2)}, u32[]{:S(2)}) async-start(bf16[2,16,128,512]{3,2,0,1:T(8,128)(2,1)} %copy.52), calls=%async_computation.1 | async-start | bytes 8388608 | tf_op jit(solution)/shard_map/all_to_all | solution.py:82
  335.7 8.3 %copy-start.1 = (bf16[512,512]{1,0:T(8,128)(2,1)S(1)}, bf16[512,512]{1,0:T(8,128)(2,1)}, u32[]{:S(2)}) copy-start(bf16[512,512]{1,0:T(8,128)(2,1)} %param.14) | copy-start | bytes 1572868
Sparse Core Ops, SparseCore 0:
  131.2 28.1 all-gather.1
